TPU v7x, 256 devices: a whole 4x4x8 slice. The times are simulated.
256 devices in a mesh: front: 8 (over x, core), grp: 32 (over y, z).
Axes of the slice: x: 4, y: 4, z: 8, core: 2. Of those that a mesh axis runs over, the one named last changes fastest.
Arguments:
- panel_block: bfloat16 [8, 4608, 1024], P('front', 'grp'), may hold values from -0.1796875 to 0.1796875
- trailing: float32 [8, 4608, 4608], P('front', 'grp')
- inverse: float32 [8, 1024, 1024], P('front')
- weights: float32 [8, 4608], P('front'), may hold values from -0.09375 to 0.09375
- live_size: int32 [8], P('front'), may hold values from 2304 to 4608, as said below
- column_source: int32 [8, 4608], P('front'), may hold values from 0 to 4607, each once within a row
- destination: int32 [8, 4608, 1], P('front', 'grp'), may hold values from 0 to 7; in each aligned block of 144 rows (0 to 143, 144 to 287, ..., all dimensions but the last counted through in order) at most 36 rows name the same one
- row_offset: int32 [8, 4608], P('front', 'grp'), may hold values from 0 to 143
Outputs:
- factor: float32 [8, 4608, 1024], P('front', 'grp')
- checksum: float32 [8, 4608], P('front', 'grp')
- ancestor: float32 [8, 4608, 4608], P('front', 'grp')
Inputs may be any that keep to these rules, and one draw needn't show every extreme that they name: `live_size`: each front's live size is 4608 minus a multiple of 576; one front is full. `destination`: among the 144 rows of one device at most 36 rows name the same ancestor front. `column_source`: each front's row is a permutation.
All inputs are finite; a program needn't handle non-finite values.
Results may differ from a plain program's by a relative error of at most 0.0003.
Values may be sent and summed in bfloat16 or wider, within the bound.
A program may use at most 128 MiB of HBM per device.

v0:
```python
import jax
import jax.numpy as jnp
from jax import lax
from jax.sharding import PartitionSpec as P


def place_columns(rows, source, live_count):
    keep_cols = (source < live_count).astype(jnp.float32)
    return jnp.take(rows, source, axis=1) * keep_cols[None, :]


def on_device(
    panel_block, trailing, inverse, weights, live_size, column_source, destination, row_offset
):
    highest_precision = lax.Precision.HIGHEST
    row_count = trailing.shape[1]
    col_count = trailing.shape[2]
    fronts = lax.axis_size("front")
    capacity = max(2, 2 * row_count // fronts)
    trail_rows = trailing[0]
    inverse_rows = inverse[0]
    live_count = live_size[0]
    panel_f32 = panel_block[0].astype(jnp.float32)
    factor = jnp.dot(panel_f32, inverse_rows.T, precision=highest_precision)
    update = lax.dot_general(
        factor,
        lax.all_gather(factor, "grp", axis=0, tiled=True),
        (((1,), (1,)), ((), ())),
        precision=highest_precision,
        preferred_element_type=jnp.float32,
    )
    schur_rows = trail_rows - update
    positions = jnp.arange(col_count, dtype=jnp.int32)
    colmask = (positions < live_count).astype(jnp.float32)
    masked_weights = weights[0] * colmask
    checksum = jnp.dot(schur_rows, masked_weights, precision=highest_precision)
    global_rows = lax.axis_index("grp") * row_count + jnp.arange(row_count, dtype=jnp.int32)
    live_rows = global_rows < live_count
    dest_front = destination[0, :, 0]
    front_ids = jnp.arange(fronts, dtype=jnp.int32)
    onehot = ((dest_front[:, None] == front_ids[None, :]) & live_rows[:, None]).astype(jnp.int32)
    running = jnp.cumsum(onehot, axis=0)
    slot_index = jnp.sum(onehot * (running - 1), axis=1)
    dest_live = jnp.where(live_rows, dest_front, fronts)
    row_tags = (
        jnp.full((fronts, capacity), -1.0, jnp.float32)
        .at[dest_live, slot_index]
        .set(row_offset[0].astype(jnp.float32), mode="drop")
    )
    permuted = place_columns(schur_rows, column_source[0], live_count)
    bucket = (
        jnp.zeros((fronts, capacity, col_count), jnp.float32)
        .at[dest_live, slot_index]
        .set(permuted, mode="drop")
    )
    received, received_tags = (
        lax.all_to_all(bucket, "front", split_axis=0, concat_axis=0, tiled=True),
        lax.all_to_all(row_tags, "front", split_axis=0, concat_axis=0, tiled=True),
    )
    flat_rows = received.reshape(fronts * capacity, col_count)
    flat_tags = received_tags.reshape(fronts * capacity)
    target_row = jnp.where(flat_tags < 0.0, row_count, flat_tags.astype(jnp.int32))
    ancestor = (
        jnp.zeros((row_count, col_count), jnp.float32).at[target_row].add(flat_rows, mode="drop")
    )
    return (factor[None], checksum[None], ancestor[None])


def solution(mesh):
    placed = (
        P("front", "grp", None),
        P("front", "grp", None),
        P("front", None, None),
        P("front", None),
        P("front"),
        P("front", None),
        P("front", "grp", None),
        P("front", "grp"),
    )
    return jax.shard_map(
        on_device,
        mesh=mesh,
        in_specs=placed,
        out_specs=(P("front", "grp", None), P("front", "grp"), P("front", "grp", None)),
        check_vma=False,
    )
```

profile of v0, /device:TPU:1, one launch (start us, length us, event | category | flops | bytes accessed | tf_op | source)
XLA Modules:
  0.0 366.7 jit_solution(13603879904250098993)
XLA Ops:
  7.2 0.0 copy-start
  7.2 0.0 copy-start.4
  7.2 0.0 copy-start.5
  7.2 0.0 all-gather.2.cloned.1.call-start
  7.3 0.9 copy-done
  8.1 5.4 %fusion = f32[144,1024]{1,0:T(8,128)} fusion(f32[1,1024,1024]{2,1,0:T(8,128)} %param.10, bf16[1,144,1024]{2,1,0:T(8,128)(2,1)S(1)} %copy-done), kind=kOutput, calls=%fused_computation.6 | convolution fusion | flops 1811939328 | bytes 5079040 | tf_op jit(solution)/shard_map/dot_general | solution.py:24
  13.6 0.0 all-gather.2.cloned.1.call-update
  14.3 0.6 reduce-window.6
  14.9 0.2 slice_reduce_fusion
  15.1 0.1 add_bitcast_fusion
  15.3 0.6 broadcast_in_dim.49
  15.9 22.1 %scatter_fusion = f32[8,36]{1,0:T(8,128)} fusion(f32[8,36]{1,0:T(8,128)} %broadcast_in_dim.49, s32[144]{0:T(256)S(1)} %bitcast.39, f32[144]{0:T(256)S(1)} %bitcast.45), kind=kCustom, calls=%fused_computation.1 | custom fusion | bytes 2880 | tf_op jit(solution)/shard_map/scatter | solution.py:48
  37.9 6.4 %all-to-all-start = ((f32[8,1,36]{2,1,0:T(1,128)}), f32[8,1,36]{2,1,0:T(1,128)S(1)}, u32[]{:S(2)}, u32[]{:S(2)}) async-start(f32[8,1,36]{2,1,0:T(1,128)} %bitcast.15), calls=%async_computation | async-start | bytes 8192 | tf_op jit(solution)/shard_map/all_to_all | solution.py:58
  44.4 0.1 fusion.6
  44.5 0.1 fusion.7
  44.6 123.4 %all-gather.2.cloned.1.call-done = f32[4608,1024]{1,0:T(8,128)} async-done(((f32[144,1024]{1,0:T(8,128)}), f32[4608,1024]{1,0:T(8,128)}) %all-gather.2.cloned.1.call-update) | async-done | bytes 18874384 | tf_op jit(solution)/shard_map/all_gather | solution.py:27
  168.0 23.8 %convolution_subtract_fusion = f32[144,4608]{1,0:T(8,128)S(1)} fusion(f32[144,1024]{1,0:T(8,128)} %fusion, f32[4608,1024]{1,0:T(8,128)} %all-gather.2.cloned.1.call-done, f32[1,144,4608]{2,1,0:T(8,128)} %param.9), kind=kOutput, calls=%fused_computation.4 | convolution fusion | flops 8154390528 | bytes 24772608 | tf_op jit(solution)/shard_map/dot_general | solution.py:25
  191.8 3.4 copy.17
  195.2 14.1 %gather_fusion = f32[4608,144]{1,0:T(8,128)} fusion(f32[144,4608]{0,1:T(8,128)} %copy.17, s32[5120]{0:T(1024)S(1)} %pad_clamp_fusion), kind=kCustom, calls=%fused_computation | custom fusion | bytes 5326848 | tf_op jit(solution)/shard_map/jit(_take)/gather | solution.py:9
  209.3 6.4 %multiply_bitcast_fusion = f32[144,4608]{0,1:T(8,128)} fusion(f32[4608,144]{1,0:T(8,128)} %gather_fusion, f32[4608]{0:T(1024)S(1)} %fusion.7, pred[4608]{0:T(1024)(128)(4,1)S(1)} %compare_and_fusion), kind=kLoop, calls=%fused_computation.5 | loop fusion | flops 1327104 | bytes 5331456 | tf_op jit(solution)/shard_map/mul | solution.py:9
  215.7 5.3 %copy.18 = f32[144,4608]{1,0:T(8,128)} copy(f32[144,4608]{0,1:T(8,128)} %multiply_bitcast_fusion) | data formatting | bytes 5308416 | tf_op jit(solution)/shard_map/mul | solution.py:9
  221.0 3.0 broadcast_in_dim.53
  224.0 39.0 %scatter_fusion.1 = f32[8,36,4608]{2,0,1:T(8,128)} fusion(f32[8,36,4608]{2,0,1:T(8,128)} %broadcast_in_dim.53, s32[144]{0:T(256)S(1)} %bitcast.40, f32[144,4608]{1,0:T(8,128)} %copy.18), kind=kCustom, calls=%fused_computation.2 | custom fusion | bytes 7963776 | tf_op jit(solution)/shard_map/scatter | solution.py:54
  263.0 8.1 %copy.19 = f32[8,36,4608]{2,1,0:T(8,128)} copy(f32[8,36,4608]{2,0,1:T(8,128)} %scatter_fusion.1) | data formatting | bytes 10616832 | tf_op jit(solution)/shard_map/scatter | solution.py:54
  271.1 0.0 all-to-all-done
  271.1 5.4 %all-to-all-start.1 = ((f32[8,36,4608]{2,1,0:T(8,128)}), f32[8,36,4608]{2,1,0:T(8,128)}, u32[]{:S(2)}, u32[]{:S(2)}) async-start(f32[8,36,4608]{2,1,0:T(8,128)} %copy.19), calls=%async_computation.1 | async-start | bytes 11796480 | tf_op jit(solution)/shard_map/all_to_all | solution.py:57
  276.7 0.1 select_n.81
  276.8 0.0 copy-start.1
  276.8 2.7 fusion.15
  279.5 64.2 %all-to-all-done.1 = f32[8,36,4608]{2,1,0:T(8,128)} async-done(((f32[8,36,4608]{2,1,0:T(8,128)}), f32[8,36,4608]{2,1,0:T(8,128)}, u32[]{:S(2)}, u32[]{:S(2)}) %all-to-all-start.1) | async-done | bytes 5308448 | tf_op jit(solution)/shard_map/all_to_all | solution.py:57
  343.7 5.6 %reshape.169 = f32[288,4608]{1,0:T(8,128)} reshape(f32[8,36,4608]{2,1,0:T(8,128)} %all-to-all-done.1) | data formatting | bytes 10616832 | tf_op jit(solution)/shard_map/reshape | solution.py:60
  349.3 10.6 %scatter_custom_fusion.2 = f32[144,4608]{1,0:T(8,128)} fusion(s32[288]{0:T(512)S(1)} %fusion.13, f32[288,4608]{1,0:T(8,128)} %reshape.169, f32[]{:T(128)} %constant.13.clone.1), kind=kCustom, calls=%fused_computation.8 | custom fusion | flops 1327104 | bytes 2654720 | tf_op jit(solution)/shard_map/scatter-add | solution.py:64
  (23 shorter events, 0.3 us)
Async XLA Ops:
  7.2 1.0 copy-start
  7.2 7.1 %copy-start.4 = (s32[1,144,1]{1,2,0:T(1,128)S(1)}, s32[1,144,1]{1,2,0:T(1,128)}, u32[]{:S(2)}) copy-start(s32[1,144,1]{1,2,0:T(1,128)} %param.14) | copy-start | bytes 1732
  7.2 7.9 %copy-start.5 = (s32[1,144]{1,0:T(1,128)S(1)}, s32[1,144]{1,0:T(1,128)}, u32[]{:S(2)}) copy-start(s32[1,144]{1,0:T(1,128)} %param.15) | copy-start | bytes 1732
  7.2 37.2 %copy-start.2 = (s32[1,4608]{1,0:T(1,128)S(1)}, s32[1,4608]{1,0:T(1,128)}, u32[]{:S(2)}) copy-start(s32[1,4608]{1,0:T(1,128)} %param.13) | copy-start | bytes 55300
  7.2 160.8 %all-gather.2.cloned.1.call-start = ((), (), s32[]{:S(2)}) async-start(), calls=%async_computation.2 | async-start | bytes 19464192 | tf_op jit(solution)/shard_map/all_gather | solution.py:27
  37.9 233.2 %all-to-all-start = ((f32[8,1,36]{2,1,0:T(1,128)}), f32[8,1,36]{2,1,0:T(1,128)S(1)}, u32[]{:S(2)}, u32[]{:S(2)}) async-start(f32[8,1,36]{2,1,0:T(1,128)} %bitcast.15), calls=%async_computation | async-start | bytes 8192 | tf_op jit(solution)/shard_map/all_to_all | solution.py:58
  271.1 5.4 %copy-start.3 = (f32[1,4608]{1,0:T(1,128)S(1)}, f32[1,4608]{1,0:T(1,128)}, u32[]{:S(2)}) copy-start(f32[1,4608]{1,0:T(1,128)} %param.11) | copy-start | bytes 55300
  271.1 72.6 %all-to-all-start.1 = ((f32[8,36,4608]{2,1,0:T(8,128)}), f32[8,36,4608]{2,1,0:T(8,128)}, u32[]{:S(2)}, u32[]{:S(2)}) async-start(f32[8,36,4608]{2,1,0:T(8,128)} %copy.19), calls=%async_computation.1 | async-start | bytes 11796480 | tf_op jit(solution)/shard_map/all_to_all | solution.py:57
  276.8 83.1 %copy-start.1 = (bf16[1,144,1024]{2,1,0:T(8,128)(2,1)S(1)}, bf16[1,144,1024]{2,1,0:T(8,128)(2,1)}, u32[]{:S(2)}) copy-start(bf16[1,144,1024]{2,1,0:T(8,128)(2,1)} %param.8) | copy-start | bytes 884740
Sparse Core Ops, SparseCore 0:
  13.7 154.2 all-gather.1
where the time goes:
time: 368 us; the launch traced here: 367 us
  waiting for transfers between devices  188 us (51%)
  local copies, waits for them, and re-layouts  102 us (28%)
  matrix products  31.9 us (9%)
  other arithmetic  18 us (5%)
  between operations  14.8 us (4%)
  starting transfers between devices  11.9 us (3%)
    all_gather x1, waiting for transfers between devices, on_device(): lax.all_gather(factor, 'grp', axis=0, tiled=True)  123 us
    all_to_all x1, waiting for transfers between devices, on_device(): lax.all_to_all(bucket, 'front', split_axis=0, concat_axis=0, tiled=True)  64.2 us
    scatter x2, local copies, waits for them, and re-layouts, on_device(): bucket = jnp.zeros((fronts, capacity, col_count), jnp.float32).at[dest_li...  47.1 us
    dot_general x1, matrix products, on_device(): lax.dot_general(factor, lax.all_gather(factor, 'grp', axis=0, tiled=True)...  23.8 us
    scatter x1, local copies, waits for them, and re-layouts, on_device(): row_tags = jnp.full((fronts, capacity), -1.0, jnp.float32).at[dest_live,...  22.1 us
    gather x1, local copies, waits for them, and re-layouts, place_columns(): return jnp.take(rows, source, axis=1) * keep_cols[None, :]  14.1 us
    scatter-add x1, other arithmetic, on_device(): jnp.zeros((row_count, col_count), jnp.float32).at[target_row]  10.6 us
  transfers between devices with their start and end apart: 3, of which 2 were waited for; matrix products, arithmetic and copies ran while one was open for 35% of the time, Pallas kernels for 0%

commit v1 on v0

--- a/solution.py
+++ b/solution.py
@@ -2,6 +2,12 @@
 import jax.numpy as jnp
 from jax import lax
 from jax.sharding import PartitionSpec as P
+
+
+def tiled_gather(x, axis, dim):
+    size = lax.axis_size(axis)
+    repeats = [size if d == dim else 1 for d in range(x.ndim)]
+    return lax.all_to_all(jnp.tile(x, repeats), axis, split_axis=dim, concat_axis=dim, tiled=True)
 
 
 def place_columns(rows, source, live_count):
@@ -24,7 +30,7 @@
     factor = jnp.dot(panel_f32, inverse_rows.T, precision=highest_precision)
     update = lax.dot_general(
         factor,
-        lax.all_gather(factor, "grp", axis=0, tiled=True),
+        tiled_gather(factor, "grp", 0),
         (((1,), (1,)), ((), ())),
         precision=highest_precision,
         preferred_element_type=jnp.float32,

time: 368 us -> 682 us (1.85)
  the two profiles are of different devices: /device:TPU:1 before, /device:TPU:184 now
where the time goes in v1:
time: 682 us; the launch traced here: 680 us
  waiting for transfers between devices  503 us (74%)
  local copies, waits for them, and re-layouts  108 us (16%)
  matrix products  31.1 us (5%)
  starting transfers between devices  18.7 us (3%)
  other arithmetic  18 us (3%)
    all_to_all x1, waiting for transfers between devices, tiled_gather(): lax.all_to_all(jnp.tile(x, repeats), axis, split_axis=dim, concat_axis=di...  438 us
    all_to_all x1, waiting for transfers between devices, on_device(): lax.all_to_all(bucket, 'front', split_axis=0, concat_axis=0, tiled=True)  65.1 us
    scatter x2, local copies, waits for them, and re-layouts, on_device(): bucket = jnp.zeros((fronts, capacity, col_count), jnp.float32).at[dest_li...  49.1 us
    dot_general x1, matrix products, on_device(): lax.dot_general(factor, tiled_gather(factor, 'grp', 0), (((1,), (1,)), ((...  23.7 us
    scatter x1, local copies, waits for them, and re-layouts, on_device(): row_tags = jnp.full((fronts, capacity), -1.0, jnp.float32).at[dest_live,...  17 us
    gather x1, local copies, waits for them, and re-layouts, place_columns(): return jnp.take(rows, source, axis=1) * keep_cols[None, :]  14.1 us
  transfers between devices with their start and end apart: 3, of which 2 were waited for; matrix products, arithmetic and copies ran while one was open for 19% of the time, Pallas kernels for 0%

profile of v1, /device:TPU:184, one launch (start us, length us, event | category | flops | bytes accessed | tf_op | source)
XLA Modules:
  0.0 680.1 jit_solution(12196984543663282156)
XLA Ops:
  0.6 0.0 copy-start
  0.6 1.0 copy-done
  1.6 4.6 fusion
  6.2 0.0 copy-start.2
  6.2 8.9 %tile.2 = f32[32,144,1024]{2,1,0:T(8,128)} broadcast(f32[144,1024]{1,0:T(8,128)S(1)} %fusion), dimensions={1,2} | broadcast | bytes 19464192 | tf_op jit(solution)/shard_map/tile | solution.py:10
  15.1 9.5 %all-to-all-start = ((f32[32,144,1024]{2,1,0:T(8,128)}), f32[32,144,1024]{2,1,0:T(8,128)}, u32[]{:S(2)}, u32[]{:S(2)}) async-start(f32[32,144,1024]{2,1,0:T(8,128)} %tile.2), calls=%async_computation | async-start | bytes 37748736 | tf_op jit(solution)/shard_map/all_to_all | solution.py:10
  25.3 0.0 copy-done.5
  25.3 0.6 reduce-window.6
  25.9 0.2 slice_reduce_fusion
  26.2 0.1 add_bitcast_fusion
  26.3 0.6 broadcast_in_dim.49
  26.9 17.0 %scatter_fusion = f32[8,36]{1,0:T(8,128)} fusion(f32[8,36]{1,0:T(8,128)} %broadcast_in_dim.49, s32[144]{0:T(256)S(1)} %bitcast.40, f32[144]{0:T(256)S(1)} %bitcast.46), kind=kCustom, calls=%fused_computation.1 | custom fusion | bytes 2880 | tf_op jit(solution)/shard_map/scatter | solution.py:54
  43.9 0.1 fusion.6
  44.0 0.1 fusion.7
  44.1 437.6 %all-to-all-done = f32[32,144,1024]{2,1,0:T(8,128)} async-done(((f32[32,144,1024]{2,1,0:T(8,128)}), f32[32,144,1024]{2,1,0:T(8,128)}, u32[]{:S(2)}, u32[]{:S(2)}) %all-to-all-start) | async-done | bytes 18874400 | tf_op jit(solution)/shard_map/all_to_all | solution.py:10
  481.7 4.3 all-to-all-start.1
  486.0 23.7 %convolution_subtract_fusion = f32[144,4608]{1,0:T(8,128)S(1)} fusion(f32[144,1024]{1,0:T(8,128)S(1)} %fusion, f32[4608,1024]{1,0:T(8,128)} %bitcast.4, f32[1,144,4608]{2,1,0:T(8,128)} %param.9), kind=kOutput, calls=%fused_computation.4 | convolution fusion | flops 8154390528 | bytes 24772608 | tf_op jit(solution)/shard_map/dot_general | solution.py:31
  509.7 3.4 copy.17
  513.1 14.1 %gather_fusion = f32[4608,144]{1,0:T(8,128)} fusion(f32[144,4608]{0,1:T(8,128)} %copy.17, s32[5120]{0:T(1024)S(1)} %pad_clamp_fusion), kind=kCustom, calls=%fused_computation | custom fusion | bytes 5326848 | tf_op jit(solution)/shard_map/jit(_take)/gather | solution.py:15
  527.2 6.4 multiply_bitcast_fusion
  533.7 5.3 copy.18
  538.9 3.0 broadcast_in_dim.53
  541.9 41.0 %scatter_fusion.1 = f32[8,36,4608]{2,0,1:T(8,128)} fusion(f32[8,36,4608]{2,0,1:T(8,128)} %broadcast_in_dim.53, s32[144]{0:T(256)S(1)} %bitcast.41, f32[144,4608]{1,0:T(8,128)} %copy.18), kind=kCustom, calls=%fused_computation.2 | custom fusion | bytes 7963776 | tf_op jit(solution)/shard_map/scatter | solution.py:60
  582.9 8.1 %copy.19 = f32[8,36,4608]{2,1,0:T(8,128)} copy(f32[8,36,4608]{2,0,1:T(8,128)} %scatter_fusion.1) | data formatting | bytes 10616832 | tf_op jit(solution)/shard_map/scatter | solution.py:60
  591.0 0.0 all-to-all-done.1
  591.0 4.9 all-to-all-start.2
  596.1 0.1 select_n.81
  596.2 0.0 copy-start.1
  596.2 2.7 fusion.15
  598.9 65.1 %all-to-all-done.2 = f32[8,36,4608]{2,1,0:T(8,128)} async-done(((f32[8,36,4608]{2,1,0:T(8,128)}), f32[8,36,4608]{2,1,0:T(8,128)}, u32[]{:S(2)}, u32[]{:S(2)}) %all-to-all-start.2) | async-done | bytes 5308448 | tf_op jit(solution)/shard_map/all_to_all | solution.py:63
  664.0 5.6 reshape.176
  669.6 10.6 %scatter_custom_fusion.2 = f32[144,4608]{1,0:T(8,128)} fusion(s32[288]{0:T(512)S(1)} %fusion.13, f32[288,4608]{1,0:T(8,128)} %reshape.176, f32[]{:T(128)} %constant.13.clone.1), kind=kCustom, calls=%fused_computation.8 | custom fusion | flops 1327104 | bytes 2654720 | tf_op jit(solution)/shard_map/scatter-add | solution.py:70
  (25 shorter events, 0.3 us)
Async XLA Ops:
  0.6 1.0 copy-start
  6.2 479.8 %copy-start.2 = (f32[144,1024]{1,0:T(8,128)}, f32[144,1024]{1,0:T(8,128)S(1)}, u32[]{:S(2)}) copy-start(f32[144,1024]{1,0:T(8,128)S(1)} %fusion) | copy-start | bytes 1769476
  15.1 10.1 %copy-start.5 = (s32[1,144,1]{1,2,0:T(1,128)S(1)}, s32[1,144,1]{1,2,0:T(1,128)}, u32[]{:S(2)}) copy-start(s32[1,144,1]{1,2,0:T(1,128)} %param.14) | copy-start | bytes 1732
  15.1 11.0 %copy-start.6 = (s32[1,144]{1,0:T(1,128)S(1)}, s32[1,144]{1,0:T(1,128)}, u32[]{:S(2)}) copy-start(s32[1,144]{1,0:T(1,128)} %param.15) | copy-start | bytes 1732
  15.1 11.0 %copy-start.3 = (s32[1,4608]{1,0:T(1,128)S(1)}, s32[1,4608]{1,0:T(1,128)}, u32[]{:S(2)}) copy-start(s32[1,4608]{1,0:T(1,128)} %param.13) | copy-start | bytes 55300
  15.1 466.6 %all-to-all-start = ((f32[32,144,1024]{2,1,0:T(8,128)}), f32[32,144,1024]{2,1,0:T(8,128)}, u32[]{:S(2)}, u32[]{:S(2)}) async-start(f32[32,144,1024]{2,1,0:T(8,128)} %tile.2), calls=%async_computation | async-start | bytes 37748736 | tf_op jit(solution)/shard_map/all_to_all | solution.py:10
  481.7 109.3 %all-to-all-start.1 = ((f32[8,1,36]{2,1,0:T(1,128)}), f32[8,1,36]{2,1,0:T(1,128)S(1)}, u32[]{:S(2)}, u32[]{:S(2)}) async-start(f32[8,1,36]{2,1,0:T(1,128)} %bitcast.16), calls=%async_computation.1 | async-start | bytes 8192 | tf_op jit(solution)/shard_map/all_to_all | solution.py:64
  591.0 4.9 copy-start.4
  591.0 73.0 %all-to-all-start.2 = ((f32[8,36,4608]{2,1,0:T(8,128)}), f32[8,36,4608]{2,1,0:T(8,128)}, u32[]{:S(2)}, u32[]{:S(2)}) async-start(f32[8,36,4608]{2,1,0:T(8,128)} %copy.19), calls=%async_computation.2 | async-start | bytes 11796480 | tf_op jit(solution)/shard_map/all_to_all | solution.py:63
  596.2 83.9 %copy-start.1 = (bf16[1,144,1024]{2,1,0:T(8,128)(2,1)S(1)}, bf16[1,144,1024]{2,1,0:T(8,128)(2,1)}, u32[]{:S(2)}) copy-start(bf16[1,144,1024]{2,1,0:T(8,128)(2,1)} %param.8) | copy-start | bytes 884740
